TPU v7x, 32 devices: a whole 2x2x4 slice. The times are simulated.
32 devices in a mesh: dp: 8 (over z, y), tp: 4 (over x, core).
Axes of the slice: x: 2, y: 2, z: 4, core: 2. Of those that a mesh axis runs over, the one named last changes fastest.
Arguments:
- hidden_in: bfloat16 [2, 8192, 1024], P(None, ('dp', 'tp')), may hold values from -6 to 6
- out_grad: bfloat16 [2, 8192, 1024], P(None, ('dp', 'tp')), may hold values from -6 to 6
- domain_ids: int32 [16], replicated, may hold values from 0 to 7
- domain_weights: float32 [8], replicated, may hold values from 0.5 to 2
- gain_attn: float32 [1024], P(('dp', 'tp')), may hold values from 0.1 to 1.9
- gain_mlp: float32 [1024], P(('dp', 'tp')), may hold values from 0.1 to 1.9
- w_query: bfloat16 [1024, 1024], P('dp', 'tp'), may hold values from -0.1875 to 0.1875
- w_kv: bfloat16 [1024, 256], P('dp', 'tp'), may hold values from -0.1875 to 0.1875
- w_out: bfloat16 [1024, 1024], P('tp', 'dp'), may hold values from -0.75 to 0.75
- w_gate: bfloat16 [1024, 2816], P('dp', 'tp'), may hold values from -0.1875 to 0.1875
- w_up: bfloat16 [1024, 2816], P('dp', 'tp'), may hold values from -0.1875 to 0.1875
- w_down: bfloat16 [2816, 1024], P('tp', 'dp'), may hold values from -0.109375 to 0.109375
Outputs:
- block_out: float32 [2, 8192, 1024], P(None, ('dp', 'tp'))
- input_grad: float32 [2, 8192, 1024], P(None, ('dp', 'tp'))
- gain_attn_grad: float32 [1024], P(('dp', 'tp'))
- gain_mlp_grad: float32 [1024], P(('dp', 'tp'))
- w_query_grad: float32 [1024, 1024], P('dp', 'tp')
- w_kv_grad: float32 [1024, 256], P('dp', 'tp')
- w_out_grad: float32 [1024, 1024], P('tp', 'dp')
- w_gate_grad: float32 [1024, 2816], P('dp', 'tp')
- w_up_grad: float32 [1024, 2816], P('dp', 'tp')
- w_down_grad: float32 [2816, 1024], P('tp', 'dp')
All inputs are finite; a program needn't handle non-finite values.
Results may differ from a plain program's by a relative error of at most 0.02.
Values may be sent and summed in bfloat16 or wider, within the bound.
No kernel may reach another device: no remote copies, remote signals or barrier semaphores. Data moves between devices by JAX's collectives and lax.ppermute only.
A program may use at most 192 MiB of HBM per device.

v0:
```python
import jax
import jax.numpy as jnp
from jax import lax
from jax.sharding import PartitionSpec as P

epsilon = 1e-06
neg_large = -1e30


def rope_tables(length, head_size):
    quarter = head_size // 4
    position = jnp.arange(length).astype(jnp.float32)
    frequency = 10000.0 ** (-jnp.arange(quarter).astype(jnp.float32) / quarter)
    angles = position[:, None] * frequency[None, :]
    return (jnp.cos(angles), jnp.sin(angles))


def rotate_half(values, cosine_table, sine_table):
    quarter = cosine_table.shape[-1]
    first_half = values[..., :quarter]
    paired = values[..., quarter : 2 * quarter]
    remainder = values[..., 2 * quarter :]
    return jnp.concatenate(
        [
            first_half * cosine_table - paired * sine_table,
            paired * cosine_table + first_half * sine_table,
            remainder,
        ],
        -1,
    )


def norm_forward(values, scales):
    inverse = lax.rsqrt(jnp.mean(values * values, -1, keepdims=True) + epsilon)
    unit_rows = values * inverse
    return (inverse, unit_rows, unit_rows * scales)


def norm_backward(grad_rows, inverse, unit_rows, scales):
    scaled = grad_rows * scales
    return inverse * (scaled - unit_rows * jnp.mean(scaled * unit_rows, -1, keepdims=True))


def masked_scores(query_block, key_rows, row_start):
    scores = jnp.einsum("tha,ua->htu", query_block, key_rows, preferred_element_type=jnp.float32)
    row_pos = row_start + jnp.arange(query_block.shape[0])
    col_pos = jnp.arange(key_rows.shape[0])
    return jnp.where(col_pos[None, None, :] <= row_pos[None, :, None], scores, neg_large)


def attend_forward(rotated, key_rows, value_rows):
    length = rotated.shape[0]
    block_rows = min(512, length)
    outputs = []
    totals = []
    for row_start in range(0, length, block_rows):
        scores = masked_scores(rotated[row_start : row_start + block_rows], key_rows, row_start)
        row_peak = jnp.max(scores, -1, keepdims=True)
        log_total = row_peak + jnp.log(jnp.sum(jnp.exp(scores - row_peak), -1, keepdims=True))
        probs_low = jnp.exp(scores - log_total).astype(jnp.bfloat16)
        outputs.append(
            jnp.einsum("htu,ua->tha", probs_low, value_rows, preferred_element_type=jnp.float32)
        )
        totals.append(log_total)
    return (jnp.concatenate(outputs, 0), totals)


def attend_backward(rotated, key_rows, value_rows, grad_mixed, totals):
    length = rotated.shape[0]
    block_rows = min(512, length)
    query_grads = []
    key_grad = jnp.zeros(key_rows.shape, jnp.float32)
    value_grad = jnp.zeros(value_rows.shape, jnp.float32)
    for block_idx, row_start in enumerate(range(0, length, block_rows)):
        query_block = rotated[row_start : row_start + block_rows]
        scores = masked_scores(query_block, key_rows, row_start)
        probs = jnp.exp(scores - totals[block_idx])
        probs_low = probs.astype(jnp.bfloat16)
        grad_block = grad_mixed[row_start : row_start + block_rows]
        grad_probs = jnp.einsum(
            "tha,ua->htu", grad_block, value_rows, preferred_element_type=jnp.float32
        )
        inner = jnp.sum(probs * grad_probs, -1, keepdims=True)
        grad_scores = (probs * (grad_probs - inner)).astype(jnp.bfloat16)
        query_grads.append(
            jnp.einsum("htu,ua->tha", grad_scores, key_rows, preferred_element_type=jnp.float32)
        )
        key_grad = key_grad + jnp.einsum(
            "htu,tha->ua", grad_scores, query_block, preferred_element_type=jnp.float32
        )
        value_grad = value_grad + jnp.einsum(
            "htu,tha->ua", probs_low, grad_block, preferred_element_type=jnp.float32
        )
    return (jnp.concatenate(query_grads, 0), key_grad, value_grad)


def local(
    hidden_in,
    out_grad,
    domain_ids,
    domain_weights,
    gain_attn,
    gain_mlp,
    w_query,
    w_kv,
    w_out,
    w_gate,
    w_up,
    w_down,
):
    micro = hidden_in.shape[0]
    n_data = lax.axis_size("dp")
    n_seqs = domain_ids.shape[0]
    head_size = w_kv.shape[1]
    per_group = w_query.shape[1] // head_size
    head_scale = head_size ** (-0.5)
    labels = jnp.arange(domain_weights.shape[0], dtype=jnp.int32)
    one_hot = (domain_ids[:, None] == labels[None, :]).astype(jnp.float32)
    counts = jnp.sum(one_hot, 0)
    gain_one, gain_two = (
        lax.all_gather(gain_attn, ("dp", "tp"), axis=0, tiled=True),
        lax.all_gather(gain_mlp, ("dp", "tp"), axis=0, tiled=True),
    )
    length = hidden_in.shape[1] * lax.axis_size("tp")
    cosine_table, sine_table = rope_tables(length, head_size)
    cos_heads = cosine_table[:, None, :]
    sin_heads = sine_table[:, None, :]
    gain_grad_one = jnp.zeros(gain_one.shape, jnp.float32)
    gain_grad_two = jnp.zeros(gain_two.shape, jnp.float32)
    outputs = []
    input_grads = []
    grad_totals = None
    for micro_idx in range(micro):
        weights_now = (
            lax.all_gather(w_query, "dp", axis=0, tiled=True),
            lax.all_gather(w_kv, "dp", axis=0, tiled=True),
            lax.all_gather(w_out, "dp", axis=1, tiled=True),
            lax.all_gather(w_gate, "dp", axis=0, tiled=True),
            lax.all_gather(w_up, "dp", axis=0, tiled=True),
            lax.all_gather(w_down, "dp", axis=1, tiled=True),
        )
        query_full, kv_full, out_full, gate_full, up_full, down_full = weights_now
        tokens = hidden_in[micro_idx].astype(jnp.float32)
        seq_index = micro_idx * n_data + lax.axis_index("dp")
        domain = lax.dynamic_index_in_dim(domain_ids, seq_index, keepdims=False)
        domain_pick = (labels == domain).astype(jnp.float32)
        factor = jnp.sum(domain_pick * domain_weights) * lax.rsqrt(
            jnp.sum(domain_pick * counts) * counts.shape[0] / n_seqs
        )
        inverse_one, unit_one, normed_one = norm_forward(tokens, gain_one)
        whole_one = lax.all_gather(normed_one.astype(jnp.bfloat16), "tp", axis=0, tiled=True)
        queries = jnp.dot(whole_one, query_full, preferred_element_type=jnp.float32).reshape(
            length, per_group, head_size
        )
        rotated = (rotate_half(queries, cos_heads, sin_heads) * head_scale).astype(jnp.bfloat16)
        kv_state = jnp.dot(whole_one, kv_full, preferred_element_type=jnp.float32)
        key_rows = rotate_half(kv_state, cosine_table, sine_table).astype(jnp.bfloat16)
        value_rows = kv_state.astype(jnp.bfloat16)
        mixed_out, totals = attend_forward(rotated, key_rows, value_rows)
        mixed_low = mixed_out.astype(jnp.bfloat16).reshape(length, per_group * head_size)
        attn_sum = lax.psum_scatter(
            jnp.dot(mixed_low, out_full, preferred_element_type=jnp.float32).astype(jnp.bfloat16),
            "tp",
            scatter_dimension=0,
            tiled=True,
        ).astype(jnp.float32)
        residual = tokens + attn_sum
        inverse_two, unit_two, normed_two = norm_forward(residual, gain_two)
        whole_two = lax.all_gather(normed_two.astype(jnp.bfloat16), "tp", axis=0, tiled=True)
        gate_val = jnp.dot(whole_two, gate_full, preferred_element_type=jnp.float32)
        up_val = jnp.dot(whole_two, up_full, preferred_element_type=jnp.float32)
        sigmoid_val = jax.nn.sigmoid(gate_val)
        silu_val = gate_val * sigmoid_val
        hidden_low = (silu_val * up_val).astype(jnp.bfloat16)
        branch = lax.psum_scatter(
            jnp.dot(hidden_low, down_full, preferred_element_type=jnp.float32).astype(jnp.bfloat16),
            "tp",
            scatter_dimension=0,
            tiled=True,
        ).astype(jnp.float32)
        outputs.append(residual + branch)
        weights_later = (
            lax.all_gather(w_query, "dp", axis=0, tiled=True),
            lax.all_gather(w_kv, "dp", axis=0, tiled=True),
            lax.all_gather(w_out, "dp", axis=1, tiled=True),
            lax.all_gather(w_gate, "dp", axis=0, tiled=True),
            lax.all_gather(w_up, "dp", axis=0, tiled=True),
            lax.all_gather(w_down, "dp", axis=1, tiled=True),
        )
        query_back, kv_back, out_back, gate_back, up_back, down_back = weights_later
        grad_out = out_grad[micro_idx].astype(jnp.float32) * factor
        grad_rows = lax.all_gather(grad_out.astype(jnp.bfloat16), "tp", axis=0, tiled=True)
        grad_hidden = jnp.einsum(
            "td,fd->tf", grad_rows, down_back, preferred_element_type=jnp.float32
        )
        grad_gate = (
            grad_hidden * up_val * sigmoid_val * (1.0 + gate_val * (1.0 - sigmoid_val))
        ).astype(jnp.bfloat16)
        grad_up = (grad_hidden * silu_val).astype(jnp.bfloat16)
        down_grad = jnp.einsum(
            "tf,td->fd", hidden_low, grad_rows, preferred_element_type=jnp.float32
        )
        gate_grad = jnp.einsum(
            "td,tf->df", whole_two, grad_gate, preferred_element_type=jnp.float32
        )
        up_grad = jnp.einsum("td,tf->df", whole_two, grad_up, preferred_element_type=jnp.float32)
        normed_two_part = jnp.einsum(
            "tf,df->td", grad_gate, gate_back, preferred_element_type=jnp.float32
        ) + jnp.einsum("tf,df->td", grad_up, up_back, preferred_element_type=jnp.float32)
        grad_normed_two = lax.psum_scatter(
            normed_two_part.astype(jnp.bfloat16), "tp", scatter_dimension=0, tiled=True
        ).astype(jnp.float32)
        gain_grad_two = gain_grad_two + jnp.sum(grad_normed_two * unit_two, 0)
        grad_residual = grad_out + norm_backward(grad_normed_two, inverse_two, unit_two, gain_two)
        grad_attn = lax.all_gather(grad_residual.astype(jnp.bfloat16), "tp", axis=0, tiled=True)
        out_grad_part = jnp.einsum(
            "tq,td->qd", mixed_low, grad_attn, preferred_element_type=jnp.float32
        )
        grad_mixed = jnp.einsum(
            "td,qd->tq", grad_attn, out_back, preferred_element_type=jnp.float32
        )
        grad_mixed = grad_mixed.astype(jnp.bfloat16).reshape(length, per_group, head_size)
        grad_rotated, key_grad, value_grad = attend_backward(
            rotated, key_rows, value_rows, grad_mixed, totals
        )
        grad_query = (rotate_half(grad_rotated, cos_heads, -sin_heads) * head_scale).astype(
            jnp.bfloat16
        )
        grad_query = grad_query.reshape(length, per_group * head_size)
        grad_kv = (value_grad + rotate_half(key_grad, cosine_table, -sine_table)).astype(
            jnp.bfloat16
        )
        query_grad = jnp.einsum(
            "td,tq->dq", whole_one, grad_query, preferred_element_type=jnp.float32
        )
        kv_grad = jnp.einsum("td,tk->dk", whole_one, grad_kv, preferred_element_type=jnp.float32)
        normed_one_part = jnp.einsum(
            "tq,dq->td", grad_query, query_back, preferred_element_type=jnp.float32
        ) + jnp.einsum("tk,dk->td", grad_kv, kv_back, preferred_element_type=jnp.float32)
        grad_normed_one = lax.psum_scatter(
            normed_one_part.astype(jnp.bfloat16), "tp", scatter_dimension=0, tiled=True
        ).astype(jnp.float32)
        gain_grad_one = gain_grad_one + jnp.sum(grad_normed_one * unit_one, 0)
        input_grads.append(
            grad_residual + norm_backward(grad_normed_one, inverse_one, unit_one, gain_one)
        )
        grads_now = (query_grad, kv_grad, out_grad_part, gate_grad, up_grad, down_grad)
        if micro_idx == 0:
            grad_totals = grads_now
        else:
            grad_totals = tuple((total + grad for total, grad in zip(grad_totals, grads_now)))
    query_total, kv_total, out_total, gate_total, up_total, down_total = grad_totals
    final_grads = (
        lax.psum_scatter(query_total, "dp", scatter_dimension=0, tiled=True),
        lax.psum_scatter(kv_total, "dp", scatter_dimension=0, tiled=True),
        lax.psum_scatter(out_total, "dp", scatter_dimension=1, tiled=True),
        lax.psum_scatter(gate_total, "dp", scatter_dimension=0, tiled=True),
        lax.psum_scatter(up_total, "dp", scatter_dimension=0, tiled=True),
        lax.psum_scatter(down_total, "dp", scatter_dimension=1, tiled=True),
    )
    gain_one_shard, gain_two_shard = (
        lax.psum_scatter(gain_grad_one, ("dp", "tp"), scatter_dimension=0, tiled=True),
        lax.psum_scatter(gain_grad_two, ("dp", "tp"), scatter_dimension=0, tiled=True),
    )
    return (
        jnp.stack(outputs, 0),
        jnp.stack(input_grads, 0),
        gain_one_shard,
        gain_two_shard,
        final_grads[0],
        final_grads[1],
        final_grads[2],
        final_grads[3],
        final_grads[4],
        final_grads[5],
    )


def solution(mesh):
    return jax.shard_map(
        local,
        mesh=mesh,
        in_specs=(
            P(None, ("dp", "tp"), None),
            P(None, ("dp", "tp"), None),
            P(),
            P(),
            P(("dp", "tp")),
            P(("dp", "tp")),
            P("dp", "tp"),
            P("dp", "tp"),
            P("tp", "dp"),
            P("dp", "tp"),
            P("dp", "tp"),
            P("tp", "dp"),
        ),
        out_specs=(
            P(None, ("dp", "tp"), None),
            P(None, ("dp", "tp"), None),
            P(("dp", "tp")),
            P(("dp", "tp")),
            P("dp", "tp"),
            P("dp", "tp"),
            P("tp", "dp"),
            P("dp", "tp"),
            P("dp", "tp"),
            P("tp", "dp"),
        ),
        check_vma=False,
    )
```

profile of v0, /device:TPU:0, one launch (start us, length us, event | category | flops | bytes accessed | tf_op | source)
XLA Modules:
  0.0 1190.9 jit_solution(2056927915261358699)
XLA Ops:
  11.3 42.1 %all-reduce.5 = (f32[1024]{0:T(1024)S(1)}, f32[1024]{0:T(1024)S(1)}) all-reduce(f32[1024]{0:T(1024)S(1)} %dynamic-update-slice, f32[1024]{0:T(1024)S(1)} %dynamic-update-slice.1), channel_id=1, replica_groups=mesh['dp'=8,'tp'=4] {'dp','tp'}, use_global_device_ids=true, to_apply=%add | all-reduce | flops 2048 | bytes 16384
  56.7 26.1 %all_gather.68 = bf16[1024,64]{0,1:T(8,128)(2,1)S(1)} all-gather(bf16[128,64]{0,1:T(8,128)(2,1)S(1)} %copy-done.81), channel_id=1, replica_groups=mesh['dp'=8,'tp'=4] {'dp'}, dimensions={0}, use_global_device_ids=true | all-gather | bytes 147456 | tf_op jit(solution)/shard_map/all_gather | solution.py:136
  83.0 33.3 %all_gather.69 = bf16[1024,256]{1,0:T(8,128)(2,1)} all-gather(bf16[128,256]{1,0:T(8,128)(2,1)S(1)} %copy-done.67), channel_id=1, replica_groups=mesh['dp'=8,'tp'=4] {'dp'}, dimensions={0}, use_global_device_ids=true | all-gather | bytes 589824 | tf_op jit(solution)/shard_map/all_gather | solution.py:135
  116.4 28.1 %all_gather.70 = bf16[256,1024]{1,0:T(8,128)(2,1)} all-gather(bf16[256,128]{1,0:T(8,128)(2,1)S(1)} %copy-done.68), channel_id=1, replica_groups=mesh['dp'=8,'tp'=4] {'dp'}, dimensions={1}, use_global_device_ids=true | all-gather | bytes 589824 | tf_op jit(solution)/shard_map/all_gather | solution.py:137
  193.9 13.0 %reduce-scatter.15.cloned.1.call-done = bf16[256,1024]{1,0:T(8,128)(2,1)} async-done(((bf16[1024,1024]{1,0:T(8,128)(2,1)}), bf16[256,1024]{1,0:T(8,128)(2,1)}) %reduce-scatter.15.cloned.1.call-update) | async-done | bytes 524304 | tf_op jit(solution)/shard_map/reduce_scatter | solution.py:161
  206.9 34.6 %reduce-scatter.19.cloned.1.call-done = bf16[256,1024]{1,0:T(8,128)(2,1)} async-done(((bf16[1024,1024]{1,0:T(8,128)(2,1)}), bf16[256,1024]{1,0:T(8,128)(2,1)}) %reduce-scatter.19.cloned.1.call-update) | async-done | bytes 524304 | tf_op jit(solution)/shard_map/reduce_scatter | solution.py:161
  273.5 39.8 %all-gather.16.cloned.1.call-done = bf16[1024,704]{0,1:T(8,128)(2,1)} async-done(((bf16[128,704]{0,1:T(8,128)(2,1)}), bf16[1024,704]{0,1:T(8,128)(2,1)}) %all-gather.16.cloned.1.call-update) | async-done | bytes 1441808 | tf_op jit(solution)/shard_map/all_gather | solution.py:138
  318.6 38.1 %all-gather.20.cloned.1.call-done = bf16[704,1024]{1,0:T(8,128)(2,1)} async-done(((bf16[704,128]{1,0:T(8,128)(2,1)}), bf16[704,1024]{1,0:T(8,128)(2,1)}) %all-gather.20.cloned.1.call-update) | async-done | bytes 1441808 | tf_op jit(solution)/shard_map/all_gather | solution.py:140
  356.8 22.3 %all-gather.30.cloned.1.call-done = bf16[1024,1024]{1,0:T(8,128)(2,1)} async-done(((bf16[256,1024]{1,0:T(8,128)(2,1)}), bf16[1024,1024]{1,0:T(8,128)(2,1)}) %all-gather.30.cloned.1.call-update) | async-done | bytes 2097168 | tf_op jit(solution)/shard_map/all_gather | solution.py:192
  412.4 23.2 %all-gather.26.cloned.1.call-done = bf16[1024,1024]{1,0:T(8,128)(2,1)} async-done(((bf16[256,1024]{1,0:T(8,128)(2,1)}), bf16[1024,1024]{1,0:T(8,128)(2,1)}) %all-gather.26.cloned.1.call-update) | async-done | bytes 2097168 | tf_op jit(solution)/shard_map/all_gather | solution.py:192
  454.3 26.2 %reduce-scatter.23.cloned.1.call-done = bf16[256,1024]{1,0:T(8,128)(2,1)} async-done(((bf16[1024,1024]{1,0:T(8,128)(2,1)}), bf16[256,1024]{1,0:T(8,128)(2,1)}) %reduce-scatter.23.cloned.1.call-update) | async-done | bytes 524304 | tf_op jit(solution)/shard_map/reduce_scatter | solution.py:210
  483.2 31.3 %reduce-scatter.21.cloned.1.call-done = bf16[256,1024]{1,0:T(8,128)(2,1)} async-done(((bf16[1024,1024]{1,0:T(8,128)(2,1)}), bf16[256,1024]{1,0:T(8,128)(2,1)}) %reduce-scatter.21.cloned.1.call-update) | async-done | bytes 524304 | tf_op jit(solution)/shard_map/reduce_scatter | solution.py:175
  518.9 21.9 %all-gather.32.cloned.1.call-done = bf16[1024,1024]{1,0:T(8,128)(2,1)} async-done(((bf16[256,1024]{1,0:T(8,128)(2,1)}), bf16[1024,1024]{1,0:T(8,128)(2,1)}) %all-gather.32.cloned.1.call-update) | async-done | bytes 2097168 | tf_op jit(solution)/shard_map/all_gather | solution.py:215
  551.4 13.9 %all-gather.28.cloned.1.call-done = bf16[1024,1024]{1,0:T(8,128)(2,1)} async-done(((bf16[256,1024]{1,0:T(8,128)(2,1)}), bf16[1024,1024]{1,0:T(8,128)(2,1)}) %all-gather.28.cloned.1.call-update) | async-done | bytes 2097168 | tf_op jit(solution)/shard_map/all_gather | solution.py:215
  568.5 14.1 %fusion.9 = (f32[4,512]{1,0:T(4,128)S(1)}, f32[4,512]{1,0:T(4,128)S(1)}, f32[1024,512,4]{1,0,2:T(8,128)}) fusion(f32[1024,512,4]{1,0,2:T(8,128)} %copy-done.1, f32[4,512]{1,0:T(4,128)S(1)} %log_add_fusion.3, pred[512,1024]{0,1:T(8,128)(4,1)S(1)} %iota_compare_fusion.1, f32[1024,512,4]{1,0,2:T(8,128)} %fusion.99, f32[4,512]{1,0:T(4,128)S(1)} %log_add_fusion.1, ...), kind=kOutput, calls=%fused_computation.17 | convolution fusion | flops 285208576 | bytes 34504704 | tf_op jit(solution)/shard_map/tha,ua->htu/dot_general | solution.py:80
  582.6 14.7 %fusion.11 = (bf16[4,512,1024]{1,2,0:T(8,128)(2,1)}, bf16[4,512,1024]{1,2,0:T(8,128)(2,1)S(1)}) fusion(f32[1024,512,4]{1,0,2:T(8,128)} %get-tuple-element.108, f32[1024,512,4]{1,0,2:T(8,128)} %copy-done.1, f32[4,512]{1,0:T(4,128)S(1)} %get-tuple-element.26, f32[4,512]{1,0:T(4,128)S(1)} %log_add_fusion.3, pred[512,1024]{0,1:T(8,128)(4,1)S(1)} %iota_compare_fusion.1, ...), kind=kLoop, calls=%fused_computation.19 | loop fusion | flops 20971520 | bytes 42500096 | tf_op jit(solution)/shard_map/convert_element_type | solution.py:84
  623.3 14.8 %fusion.8 = (bf16[4,512,1024]{1,2,0:T(8,128)(2,1)S(1)}, bf16[4,512,1024]{1,2,0:T(8,128)(2,1)}) fusion(f32[1024,512,4]{1,0,2:T(8,128)} %get-tuple-element.107, f32[1024,512,4]{1,0,2:T(8,128)} %copy-done, f32[4,512]{1,0:T(4,128)S(1)} %get-tuple-element.28, f32[4,512]{1,0:T(4,128)S(1)} %log_add_fusion.2, pred[512,1024]{0,1:T(8,128)(4,1)S(1)} %iota_compare_fusion, ...), kind=kLoop, calls=%fused_computation.14 | loop fusion | flops 20971520 | bytes 42500096 | tf_op jit(solution)/shard_map/convert_element_type | solution.py:84
  723.0 39.5 %all-reduce.4 = (f32[1024]{0:T(1024)S(1)}, f32[1024]{0:T(1024)S(1)}) all-reduce(f32[1024]{0:T(1024)S(1)} %add.272, f32[1024]{0:T(1024)S(1)} %add.273), channel_id=10, replica_groups=mesh['dp'=8,'tp'=4] {'dp','tp'}, use_global_device_ids=true, to_apply=%region_35.36.clone | all-reduce | flops 2048 | bytes 16384
  771.9 59.8 %reduce-scatter.41.cloned.1.call-done = f32[704,128]{1,0:T(8,128)} async-done(((f32[704,1024]{1,0:T(8,128)}), f32[704,128]{1,0:T(8,128)}) %reduce-scatter.41.cloned.1.call-update) | async-done | bytes 360464 | tf_op jit(solution)/shard_map/reduce_scatter | solution.py:259
  831.7 76.1 %reduce-scatter.39.cloned.1.call-done = f32[128,704]{0,1:T(8,128)} async-done(((f32[1024,704]{0,1:T(8,128)}), f32[128,704]{0,1:T(8,128)}) %reduce-scatter.39.cloned.1.call-update) | async-done | bytes 360464 | tf_op jit(solution)/shard_map/reduce_scatter | solution.py:258
  907.8 76.1 %reduce-scatter.37.cloned.1.call-done = f32[128,704]{0,1:T(8,128)} async-done(((f32[1024,704]{0,1:T(8,128)}), f32[128,704]{0,1:T(8,128)}) %reduce-scatter.37.cloned.1.call-update) | async-done | bytes 360464 | tf_op jit(solution)/shard_map/reduce_scatter | solution.py:257
  983.9 65.0 %reduce-scatter.33.cloned.1.call-done = f32[128,64]{0,1:T(8,128)} async-done(((f32[1024,64]{0,1:T(8,128)}), f32[128,64]{0,1:T(8,128)}) %reduce-scatter.33.cloned.1.call-update) | async-done | bytes 32784 | tf_op jit(solution)/shard_map/reduce_scatter | solution.py:255
  1048.9 67.2 %reduce-scatter.35.cloned.1.call-done = f32[256,128]{1,0:T(8,128)} async-done(((f32[256,1024]{1,0:T(8,128)}), f32[256,128]{1,0:T(8,128)}) %reduce-scatter.35.cloned.1.call-update) | async-done | bytes 131088 | tf_op jit(solution)/shard_map/reduce_scatter | solution.py:256
  1116.0 67.0 %reduce-scatter.31.cloned.1.call-done = f32[128,256]{1,0:T(8,128)} async-done(((f32[1024,256]{1,0:T(8,128)}), f32[128,256]{1,0:T(8,128)}) %reduce-scatter.31.cloned.1.call-update) | async-done | bytes 131088 | tf_op jit(solution)/shard_map/reduce_scatter | solution.py:254
  (418 shorter events, 282.1 us)
Async XLA Ops:
  8.0 136.9 %all-gather.22.cloned.1.call-start = ((), (), s32[]{:S(2)}) async-start(), calls=%async_computation.21 | async-start | bytes 2621440 | tf_op jit(solution)/shard_map/all_gather | solution.py:151
  55.9 92.2 %all-gather.12.cloned.1.call-start = ((), (), s32[]{:S(2)}) async-start(), calls=%async_computation.14 | async-start | bytes 2621440 | tf_op jit(solution)/shard_map/all_gather | solution.py:151
  56.6 150.2 %reduce-scatter.15.cloned.1.call-start = ((), (), s32[]{:S(2)}) async-start(), calls=%async_computation.15 | async-start | bytes 2621440 | tf_op jit(solution)/shard_map/reduce_scatter | solution.py:161
  175.4 66.1 %reduce-scatter.19.cloned.1.call-start = ((), (), s32[]{:S(2)}) async-start(), calls=%async_computation.22 | async-start | bytes 2621440 | tf_op jit(solution)/shard_map/reduce_scatter | solution.py:161
  193.2 62.4 %all-gather.18.cloned.1.call-start = ((), (), s32[]{:S(2)}) async-start(), calls=%async_computation.18 | async-start | bytes 1622016 | tf_op jit(solution)/shard_map/all_gather | solution.py:139
  193.8 74.4 %all-gather.24.cloned.1.call-start = ((), (), s32[]{:S(2)}) async-start(), calls=%async_computation.23 | async-start | bytes 2621440 | tf_op jit(solution)/shard_map/all_gather | solution.py:169
  245.7 67.6 %all-gather.16.cloned.1.call-start = ((), (), s32[]{:S(2)}) async-start(), calls=%async_computation.17 | async-start | bytes 1622016 | tf_op jit(solution)/shard_map/all_gather | solution.py:138
  246.3 110.5 %all-gather.20.cloned.1.call-start = ((), (), s32[]{:S(2)}) async-start(), calls=%async_computation.19 | async-start | bytes 1622016 | tf_op jit(solution)/shard_map/all_gather | solution.py:140
  247.0 132.0 %all-gather.30.cloned.1.call-start = ((), (), s32[]{:S(2)}) async-start(), calls=%async_computation.29 | async-start | bytes 2621440 | tf_op jit(solution)/shard_map/all_gather | solution.py:192
  253.7 150.0 %all-gather.14.cloned.1.call-start = ((), (), s32[]{:S(2)}) async-start(), calls=%async_computation.16 | async-start | bytes 2621440 | tf_op jit(solution)/shard_map/all_gather | solution.py:169
  254.5 181.2 %all-gather.26.cloned.1.call-start = ((), (), s32[]{:S(2)}) async-start(), calls=%async_computation.25 | async-start | bytes 2621440 | tf_op jit(solution)/shard_map/all_gather | solution.py:192
  255.1 199.3 %reduce-scatter.27.cloned.1.call-start = ((), (), s32[]{:S(2)}) async-start(), calls=%async_computation.30 | async-start | bytes 2621440 | tf_op jit(solution)/shard_map/reduce_scatter | solution.py:210
  392.3 88.2 %reduce-scatter.23.cloned.1.call-start = ((), (), s32[]{:S(2)}) async-start(), calls=%async_computation.26 | async-start | bytes 2621440 | tf_op jit(solution)/shard_map/reduce_scatter | solution.py:210
  448.9 65.5 %reduce-scatter.21.cloned.1.call-start = ((), (), s32[]{:S(2)}) async-start(), calls=%async_computation.24 | async-start | bytes 2621440 | tf_op jit(solution)/shard_map/reduce_scatter | solution.py:175
  454.1 86.8 %all-gather.32.cloned.1.call-start = ((), (), s32[]{:S(2)}) async-start(), calls=%async_computation.31 | async-start | bytes 2621440 | tf_op jit(solution)/shard_map/all_gather | solution.py:215
  518.9 189.4 %reduce-scatter.29.cloned.1.call-start = ((), (), s32[]{:S(2)}) async-start(), calls=%async_computation.32 | async-start | bytes 2621440 | tf_op jit(solution)/shard_map/reduce_scatter | solution.py:240
  655.1 65.9 %reduce-scatter.25.cloned.1.call-start = ((), (), s32[]{:S(2)}) async-start(), calls=%async_computation.28 | async-start | bytes 2621440 | tf_op jit(solution)/shard_map/reduce_scatter | solution.py:240
  668.1 98.4 %reduce-scatter.17.cloned.1.call-start = ((), (), s32[]{:S(2)}) async-start(), calls=%async_computation.20 | async-start | bytes 2621440 | tf_op jit(solution)/shard_map/reduce_scatter | solution.py:175
  673.0 158.7 %reduce-scatter.41.cloned.1.call-start = ((), (), s32[]{:S(2)}) async-start(), calls=%async_computation.38 | async-start | bytes 3244032 | tf_op jit(solution)/shard_map/reduce_scatter | solution.py:259
  680.1 227.6 %reduce-scatter.39.cloned.1.call-start = ((), (), s32[]{:S(2)}) async-start(), calls=%async_computation.37 | async-start | bytes 3244032 | tf_op jit(solution)/shard_map/reduce_scatter | solution.py:258
  687.4 296.5 %reduce-scatter.37.cloned.1.call-start = ((), (), s32[]{:S(2)}) async-start(), calls=%async_computation.36 | async-start | bytes 3244032 | tf_op jit(solution)/shard_map/reduce_scatter | solution.py:257
  694.6 354.3 %reduce-scatter.33.cloned.1.call-start = ((), (), s32[]{:S(2)}) async-start(), calls=%async_computation.34 | async-start | bytes 294912 | tf_op jit(solution)/shard_map/reduce_scatter | solution.py:255
  699.0 417.0 %reduce-scatter.35.cloned.1.call-start = ((), (), s32[]{:S(2)}) async-start(), calls=%async_computation.35 | async-start | bytes 1179648 | tf_op jit(solution)/shard_map/reduce_scatter | solution.py:256
  703.5 479.5 %reduce-scatter.31.cloned.1.call-start = ((), (), s32[]{:S(2)}) async-start(), calls=%async_computation.33 | async-start | bytes 1179648 | tf_op jit(solution)/shard_map/reduce_scatter | solution.py:254
  (120 other events, 3226.4 us)
Sparse Core Ops, SparseCore 0:
  56.0 22.3 all-gather.21
  80.6 22.5 all-gather.11
  175.5 31.3 reduce-scatter.14
  210.0 31.4 reduce-scatter.18
  392.5 31.7 reduce-scatter.26
  449.1 31.3 reduce-scatter.22
  483.0 31.3 reduce-scatter.20
Sparse Core Ops, SparseCore 1:
  195.7 42.9 all-gather.17
  245.8 22.4 all-gather.23
  270.2 43.1 all-gather.15
  315.4 41.3 all-gather.19
  358.3 20.6 all-gather.29
  381.2 22.4 all-gather.13
  405.2 30.4 all-gather.25
  518.4 22.4 all-gather.31
  542.9 22.4 all-gather.27
  655.2 31.4 reduce-scatter.28
  689.6 31.4 reduce-scatter.24
  723.7 31.4 reduce-scatter.16
  759.2 72.4 reduce-scatter.40
  835.8 71.9 reduce-scatter.38
  911.9 71.9 reduce-scatter.36
  987.8 61.0 reduce-scatter.32
  1052.9 63.1 reduce-scatter.34
  1120.4 62.5 reduce-scatter.30
where the time goes:
time: 1200 us; the launch traced here: 1190 us
  waiting for transfers between devices  717 us (60%)
  matrix products  200 us (17%)
  blocking collectives  169 us (14%)
  other arithmetic  69.8 us (6%)
  between operations  20.6 us (2%)
  local copies, waits for them, and re-layouts  12.5 us (1%)
    unnamed x2, blocking collectives  81.5 us
    reduce_scatter x1, waiting for transfers between devices, local(): lax.psum_scatter(gate_total, 'dp', scatter_dimension=0, tiled=True)  76.1 us
    reduce_scatter x1, waiting for transfers between devices, local(): lax.psum_scatter(up_total, 'dp', scatter_dimension=0, tiled=True)  76.1 us
    reduce_scatter x1, waiting for transfers between devices, local(): lax.psum_scatter(out_total, 'dp', scatter_dimension=1, tiled=True)  67.2 us
    reduce_scatter x1, waiting for transfers between devices, local(): lax.psum_scatter(query_total, 'dp', scatter_dimension=0, tiled=True)  67 us
    reduce_scatter x1, waiting for transfers between devices, local(): lax.psum_scatter(kv_total, 'dp', scatter_dimension=0, tiled=True)  65 us
    reduce_scatter x1, waiting for transfers between devices, local(): lax.psum_scatter(down_total, 'dp', scatter_dimension=1, tiled=True)  59.8 us
    reduce_scatter x2, waiting for transfers between devices, local(): lax.psum_scatter(jnp.dot(mixed_low, out_full, preferred_element_type=jnp....  47.6 us
  transfers between devices with their start and end apart: 25, of which 19 were waited for; matrix products, arithmetic and copies ran while one was open for 13% of the time, Pallas kernels for 0%

commit v1 on v0

v1 whole, which is shorter than its diff:
```python
import jax
import jax.numpy as jnp
from jax import lax
from jax.sharding import PartitionSpec as P

epsilon = 1e-06
neg_large = -1e30
bf16 = jnp.bfloat16
f32 = jnp.float32


def rope_tables(length, head_size):
    quarter = head_size // 4
    position = jnp.arange(length).astype(f32)
    frequency = 10000.0 ** (-jnp.arange(quarter).astype(f32) / quarter)
    angles = position[:, None] * frequency[None, :]
    return (jnp.cos(angles), jnp.sin(angles))


def rotate_half(values, cosine_table, sine_table):
    quarter = cosine_table.shape[-1]
    first_half = values[..., :quarter]
    paired = values[..., quarter : 2 * quarter]
    remainder = values[..., 2 * quarter :]
    return jnp.concatenate(
        [
            first_half * cosine_table - paired * sine_table,
            paired * cosine_table + first_half * sine_table,
            remainder,
        ],
        -1,
    )


def masked_scores(query_block, key_rows, row_start):
    scores = jnp.einsum("tha,ua->htu", query_block, key_rows, preferred_element_type=f32)
    row_pos = row_start + jnp.arange(query_block.shape[0])
    col_pos = jnp.arange(key_rows.shape[0])
    return jnp.where(col_pos[None, None, :] <= row_pos[None, :, None], scores, neg_large)


def attend_forward(rotated, key_rows, value_rows):
    length = rotated.shape[0]
    block_rows = min(512, length)
    outputs = []
    totals = []
    for row_start in range(0, length, block_rows):
        scores = masked_scores(rotated[row_start : row_start + block_rows], key_rows, row_start)
        row_peak = jnp.max(scores, -1, keepdims=True)
        log_total = row_peak + jnp.log(jnp.sum(jnp.exp(scores - row_peak), -1, keepdims=True))
        probs_low = jnp.exp(scores - log_total).astype(bf16)
        outputs.append(jnp.einsum("htu,ua->tha", probs_low, value_rows, preferred_element_type=f32))
        totals.append(log_total)
    return (jnp.concatenate(outputs, 0), totals)


def attend_backward(rotated, key_rows, value_rows, grad_mixed, totals):
    length = rotated.shape[0]
    block_rows = min(512, length)
    query_grads = []
    key_grad = jnp.zeros(key_rows.shape, f32)
    value_grad = jnp.zeros(value_rows.shape, f32)
    for block_idx, row_start in enumerate(range(0, length, block_rows)):
        query_block = rotated[row_start : row_start + block_rows]
        scores = masked_scores(query_block, key_rows, row_start)
        probs = jnp.exp(scores - totals[block_idx])
        probs_low = probs.astype(bf16)
        grad_block = grad_mixed[row_start : row_start + block_rows]
        grad_probs = jnp.einsum("tha,ua->htu", grad_block, value_rows, preferred_element_type=f32)
        inner = jnp.sum(probs * grad_probs, -1, keepdims=True)
        grad_scores = (probs * (grad_probs - inner)).astype(bf16)
        query_grads.append(jnp.einsum("htu,ua->tha", grad_scores, key_rows, preferred_element_type=f32))
        key_grad = key_grad + jnp.einsum("htu,tha->ua", grad_scores, query_block, preferred_element_type=f32)
        value_grad = value_grad + jnp.einsum("htu,tha->ua", probs_low, grad_block, preferred_element_type=f32)
    return (jnp.concatenate(query_grads, 0), key_grad, value_grad)


def swap_chip(values):
    return lax.ppermute(values, "tp", [(j, j ^ 2) for j in range(4)])


def swap_core(values):
    return lax.ppermute(values, "tp", [(j, j ^ 1) for j in range(4)])


def swap_dp(values, bit):
    size = lax.axis_size("dp")
    return lax.ppermute(values, "dp", [(i, i ^ (1 << bit)) for i in range(size)])


def gather_weight(shard, order, n_bits):
    rows, cols = shard.shape
    pieces = [shard.reshape((1,) * n_bits + (rows, cols))]
    for step in order:
        if step == "x":
            pieces = pieces + [swap_chip(piece) for piece in pieces]
        else:
            pieces = [
                jnp.concatenate([piece, swap_dp(piece, step)], n_bits - 1 - step) for piece in pieces
            ]
    return [piece.reshape(-1, cols) for piece in pieces]


def scatter_grad(pair, order, n_bits):
    cols = pair[0].shape[1]
    rows = pair[0].shape[0] >> n_bits
    pieces = [piece.reshape((2,) * n_bits + (rows, cols)) for piece in pair]
    for step in order:
        if step == "x":
            pieces = [pieces[0] + swap_chip(pieces[1])]
        else:
            axis = n_bits - 1 - step
            pieces = [
                lax.slice_in_dim(piece, 0, 1, axis=axis)
                + swap_dp(lax.slice_in_dim(piece, 1, 2, axis=axis), step)
                for piece in pieces
            ]
    return pieces[0].reshape(rows, cols)


def nt(left, right):
    return lax.dot_general(left, right, (((1,), (1,)), ((), ())), preferred_element_type=f32)


def tn(left, right):
    return lax.dot_general(left, right, (((0,), (0,)), ((), ())), preferred_element_type=f32)


def nn(left, right):
    return jnp.dot(left, right, preferred_element_type=f32)


def xor_columns(values, index, n_blocks):
    shape = values.shape
    blocks = values.reshape(shape[:-1] + (n_blocks, shape[-1] // n_blocks))
    picks = jnp.arange(n_blocks, dtype=jnp.int32) ^ index
    return jnp.take(blocks, picks, axis=-2).reshape(shape)


def local(
    hidden_in,
    out_grad,
    domain_ids,
    domain_weights,
    gain_attn,
    gain_mlp,
    w_query,
    w_kv,
    w_out,
    w_gate,
    w_up,
    w_down,
):
    n_dp = lax.axis_size("dp")
    n_bits = n_dp.bit_length() - 1
    n_seqs = domain_ids.shape[0]
    head_size = w_kv.shape[1]
    per_group = w_query.shape[1] // head_size
    head_scale = head_size ** (-0.5)
    _, block, width = hidden_in.shape
    length = 4 * block
    dp_index = lax.axis_index("dp")
    tp_index = lax.axis_index("tp")
    chip = tp_index // 2
    core = tp_index % 2

    high = list(range(n_bits - 1, 0, -1))
    order_a = high + [0, "x"]
    order_b = high + ["x", 0]
    order_c = ["x", 0] + high

    gains = jnp.stack([gain_attn, gain_mlp])
    n_own = gains.shape[1]
    padded = lax.dynamic_update_slice(
        jnp.zeros((2, 4 * n_own), f32), gains, (jnp.int32(0), tp_index * n_own)
    )
    padded = padded + swap_core(padded)
    padded = padded + swap_chip(padded)
    gain_one, gain_two = padded[0][:, None], padded[1][:, None]

    qkv_cols = [w_query.shape[1], w_kv.shape[1]]
    shard_qkv = (jnp.concatenate([w_query, w_kv], 1).astype(f32) * gain_one).astype(bf16)
    shard_out = w_out.T
    shard_gate = (w_gate.astype(f32) * gain_two).astype(bf16)
    shard_up = (w_up.astype(f32) * gain_two).astype(bf16)
    shard_down = w_down.T
    qkv_w = gather_weight(shard_qkv, order_b, n_bits)
    out_w = gather_weight(shard_out, order_c, n_bits)
    gate_w = gather_weight(shard_gate, order_b, n_bits)
    up_w = gather_weight(shard_up, order_b, n_bits)
    down_w = gather_weight(shard_down, order_c, n_bits)

    def by_chip(own, other):
        first = chip == 0
        return jnp.stack([jnp.where(first, own, other), jnp.where(first, other, own)])

    def enter(values):
        own = lax.dynamic_index_in_dim(values, chip, keepdims=False)
        other = swap_chip(lax.dynamic_index_in_dim(values, 1 - chip, keepdims=False))
        mine = xor_columns(by_chip(own, other), dp_index, n_dp)
        theirs = swap_core(mine)
        first = core == 0
        return jnp.stack(
            [jnp.where(first, mine, theirs), jnp.where(first, theirs, mine)], 1
        ).reshape(length, width)

    def core_rows(values, which):
        return lax.dynamic_index_in_dim(
            values.reshape(2, 2, block, width), which, axis=1, keepdims=False
        )

    def leave(values):
        values = xor_columns(values, dp_index, n_dp)
        own = lax.dynamic_index_in_dim(values, chip, keepdims=False)
        other = lax.dynamic_index_in_dim(values, 1 - chip, keepdims=False)
        return by_chip(own, swap_chip(other.astype(bf16)).astype(f32))

    tokens = enter(hidden_in).astype(f32)
    labels = jnp.arange(domain_weights.shape[0], dtype=jnp.int32)
    one_hot = (domain_ids[:, None] == labels[None, :]).astype(f32)
    counts = jnp.sum(one_hot, 0)
    domain = lax.dynamic_index_in_dim(domain_ids, chip * n_dp + dp_index, keepdims=False)
    domain_pick = (labels == domain).astype(f32)
    factor = jnp.sum(domain_pick * domain_weights) * lax.rsqrt(
        jnp.sum(domain_pick * counts) * counts.shape[0] / n_seqs
    )
    grad_out = enter(out_grad).astype(f32) * factor
    grad_rows = grad_out.astype(bf16)

    cosine_table, sine_table = rope_tables(length, head_size)
    cos_heads = cosine_table[:, None, :]
    sin_heads = sine_table[:, None, :]

    inverse_one = lax.rsqrt(jnp.mean(tokens * tokens, -1, keepdims=True) + epsilon)
    unit_one = tokens * inverse_one
    low_one = unit_one.astype(bf16)
    kept = []
    attn_part = 0.0
    for group in range(2):
        both = nn(low_one, qkv_w[group])
        queries = both[:, : qkv_cols[0]].reshape(length, per_group, head_size)
        kv_state = both[:, qkv_cols[0] :]
        rotated = (rotate_half(queries, cos_heads, sin_heads) * head_scale).astype(bf16)
        key_rows = rotate_half(kv_state, cosine_table, sine_table).astype(bf16)
        value_rows = kv_state.astype(bf16)
        mixed_out, totals = attend_forward(rotated, key_rows, value_rows)
        mixed_low = mixed_out.astype(bf16).reshape(length, per_group * head_size)
        kept.append((rotated, key_rows, value_rows, mixed_low, totals))
        attn_part = attn_part + nt(mixed_low, out_w[group])
    attn_part = attn_part.astype(bf16)
    residual = tokens + (attn_part.astype(f32) + swap_core(attn_part).astype(f32))

    inverse_two = lax.rsqrt(jnp.mean(residual * residual, -1, keepdims=True) + epsilon)
    unit_two = residual * inverse_two
    low_two = unit_two.astype(bf16)
    branch = 0.0
    grads_gate, grads_up, grads_down = [], [], []
    back_two = 0.0
    for piece in range(2):
        gate_val = nn(low_two, gate_w[piece])
        up_val = nn(low_two, up_w[piece])
        sigmoid_val = jax.nn.sigmoid(gate_val)
        silu_val = gate_val * sigmoid_val
        hidden_low = (silu_val * up_val).astype(bf16)
        branch = branch + nt(hidden_low, down_w[piece])
        grads_down.append(tn(grad_rows, hidden_low).astype(bf16))
        grad_hidden = nn(grad_rows, down_w[piece])
        grad_gate = (
            grad_hidden * up_val * sigmoid_val * (1.0 + gate_val * (1.0 - sigmoid_val))
        ).astype(bf16)
        grad_up = (grad_hidden * silu_val).astype(bf16)
        grads_gate.append(tn(low_two, grad_gate).astype(bf16))
        grads_up.append(tn(low_two, grad_up).astype(bf16))
        back_two = back_two + nt(grad_gate, gate_w[piece]) + nt(grad_up, up_w[piece])
    branch = branch.astype(bf16)
    branch_rows = core_rows(branch, core).astype(f32) + swap_core(core_rows(branch, 1 - core)).astype(f32)
    block_out = leave(core_rows(residual, core) + branch_rows)

    back_two = back_two.astype(bf16)
    scaled_two = back_two.astype(f32) + swap_core(back_two).astype(f32)
    grad_residual = grad_out + inverse_two * (
        scaled_two - unit_two * jnp.mean(scaled_two * unit_two, -1, keepdims=True)
    )
    grad_attn = grad_residual.astype(bf16)

    down_sum = scatter_grad(grads_down, order_c[::-1], n_bits)
    gate_sum = scatter_grad(grads_gate, order_a[::-1], n_bits)
    up_sum = scatter_grad(grads_up, order_b[::-1], n_bits)

    back_one = 0.0
    grads_qkv, grads_out = [], []
    for group in range(2):
        rotated, key_rows, value_rows, mixed_low, totals = kept[group]
        grads_out.append(tn(grad_attn, mixed_low).astype(bf16))
        grad_mixed = nn(grad_attn, out_w[group]).astype(bf16).reshape(length, per_group, head_size)
        grad_rotated, key_grad, value_grad = attend_backward(
            rotated, key_rows, value_rows, grad_mixed, totals
        )
        grad_query = (rotate_half(grad_rotated, cos_heads, -sin_heads) * head_scale).astype(bf16)
        grad_kv = (value_grad + rotate_half(key_grad, cosine_table, -sine_table)).astype(bf16)
        grad_both = jnp.concatenate([grad_query.reshape(length, -1), grad_kv], 1)
        grads_qkv.append(tn(low_one, grad_both).astype(bf16))
        back_one = back_one + nt(grad_both, qkv_w[group])
    out_sum = scatter_grad(grads_out, order_c[::-1], n_bits)
    qkv_sum = scatter_grad(grads_qkv, order_b[::-1], n_bits)
    back_one = back_one.astype(bf16)
    scaled_one = core_rows(back_one, core).astype(f32) + swap_core(core_rows(back_one, 1 - core)).astype(f32)
    unit_rows = core_rows(unit_one, core)
    inverse_rows = lax.dynamic_index_in_dim(
        inverse_one.reshape(2, 2, block, 1), core, axis=1, keepdims=False
    )
    input_grad = leave(
        core_rows(grad_residual, core)
        + inverse_rows * (scaled_one - unit_rows * jnp.mean(scaled_one * unit_rows, -1, keepdims=True))
    )

    query_sum = qkv_sum[:, : qkv_cols[0]].astype(f32)
    kv_sum = qkv_sum[:, qkv_cols[0] :].astype(f32)
    gate_sum, up_sum = gate_sum.astype(f32), up_sum.astype(f32)
    gain_grads = jnp.stack(
        [
            jnp.sum(query_sum * w_query.astype(f32), 1) + jnp.sum(kv_sum * w_kv.astype(f32), 1),
            jnp.sum(gate_sum * w_gate.astype(f32), 1) + jnp.sum(up_sum * w_up.astype(f32), 1),
        ]
    )
    gain_grads = gain_grads + swap_core(gain_grads)
    gain_grads = gain_grads + swap_chip(gain_grads)
    gain_grads = lax.dynamic_slice_in_dim(gain_grads, tp_index * n_own, n_own, axis=1)
    return (
        block_out,
        input_grad,
        gain_grads[0],
        gain_grads[1],
        query_sum * gain_one,
        kv_sum * gain_one,
        out_sum.T.astype(f32),
        gate_sum * gain_two,
        up_sum * gain_two,
        down_sum.T.astype(f32),
    )


def solution(mesh):
    rows = P(None, ("dp", "tp"), None)
    vector = P(("dp", "tp"))
    weights = (P("dp", "tp"), P("dp", "tp"), P("tp", "dp"), P("dp", "tp"), P("dp", "tp"), P("tp", "dp"))
    return jax.shard_map(
        local,
        mesh=mesh,
        in_specs=(rows, rows, P(), P(), vector, vector) + weights,
        out_specs=(rows, rows, vector, vector) + weights,
        check_vma=False,
    )
```

time: 1200 us -> 686 us (0.57)
  waiting for transfers between devices: 717 us -> 124 us
  blocking collectives: 169 us -> 0 us
  local copies, waits for them, and re-layouts: 12.5 us -> 171 us
  other arithmetic: 69.8 us -> 142 us
  starting transfers between devices: 2.63 us -> 71.9 us
  matrix products: 200 us -> 162 us
  between operations: 20.6 us -> 4.94 us
    reduce_scatter x14 -> x0, waiting for transfers between devices: 529 us -> none  [the longest x1 76.1 us: local(): lax.psum_scatter(gate_total, 'dp', scatter_dimension=0, tiled=True)]
    all_gather x11 -> x0, waiting for transfers between devices: 183 us -> none  [the longest x2 45.5 us: local(): lax.all_gather(grad_out.astype(jnp.bfloat16), 'tp', axis=0, tiled=True)]
    ppermute x0 -> x71, waiting for transfers between devices: none -> 124 us  [the longest x47 104 us: swap_dp(): return lax.ppermute(values, 'dp', [(i, i ^ 1 << bit) for i in range(size)])]
    all_gather x3 -> x0, blocking collectives: 87.5 us -> none  [the longest x1 33.3 us: local(): lax.all_gather(w_query, 'dp', axis=0, tiled=True)]
    unnamed x2 -> x0, blocking collectives: 81.5 us -> none
    ppermute x0 -> x71, starting transfers between devices: none -> 71.9 us  [the longest x47 51.5 us: swap_dp(): return lax.ppermute(values, 'dp', [(i, i ^ 1 << bit) for i in range(size)])]
    reshape x0 -> x17, local copies, waits for them, and re-layouts: none -> 40 us  [the longest x9 23 us: scatter_grad(): pieces = [piece.reshape((2,) * n_bits + (rows, cols)) for piece in pair]]
    dot_general x52 -> x46, matrix products: 158 us -> 124 us  [the longest x10 26.6 us: nt(): lax.dot_general(left, right, (((1,), (1,)), ((), ())), preferred_element_...]
  transfers between devices with their start and end apart: 25 -> 71, of which waited for: 19 -> 22; matrix products, arithmetic and copies ran while one was open for 13% -> 59% of each run, Pallas kernels for 0% -> 0%
where the time goes in v1:
time: 686 us; the launch traced here: 676 us
  local copies, waits for them, and re-layouts  171 us (25%)
  matrix products  162 us (24%)
  other arithmetic  142 us (21%)
  waiting for transfers between devices  124 us (18%)
  starting transfers between devices  71.9 us (10%)
    ppermute x47, waiting for transfers between devices, swap_dp(): return lax.ppermute(values, 'dp', [(i, i ^ 1 << bit) for i in range(size)])  104 us
    ppermute x47, starting transfers between devices, swap_dp(): return lax.ppermute(values, 'dp', [(i, i ^ 1 << bit) for i in range(size)])  51.5 us
    unnamed x388, local copies, waits for them, and re-layouts  37.1 us
    concatenate x22, other arithmetic, gather_weight(): jnp.concatenate([piece, swap_dp(piece, step)], n_bits - 1 - step)  30.2 us
    convert_element_type x2, other arithmetic, attend_backward(): grad_scores = (probs * (grad_probs - inner)).astype(bf16)  29.6 us
    dot_general x4, matrix products, attend_backward(): jnp.einsum('tha,ua->htu', grad_block, value_rows, preferred_element_type=...  28.7 us
    dot_general x10, matrix products, nt(): lax.dot_general(left, right, (((1,), (1,)), ((), ())), preferred_element_...  26.6 us
    reshape x9, local copies, waits for them, and re-layouts, scatter_grad(): pieces = [piece.reshape((2,) * n_bits + (rows, cols)) for piece in pair]  23 us
  transfers between devices with their start and end apart: 71, of which 22 were waited for; matrix products, arithmetic and copies ran while one was open for 59% of the time, Pallas kernels for 0%

profile of v1, /device:TPU:0, one launch (start us, length us, event | category | flops | bytes accessed | tf_op | source)
XLA Modules:
  0.0 676.1 jit_solution(14316206685978410114)
XLA Ops:
  49.4 13.4 %collective-permute-done.20 = bf16[1,1,1,128,704]{3,4,2,1,0:T(8,128)(2,1)S(1)} collective-permute-done((bf16[1,1,1,128,704]{3,4,2,1,0:T(8,128)(2,1)S(1)}, bf16[1,1,1,128,704]{3,4,2,1,0:T(8,128)(2,1)S(1)}, u32[]{:S(2)}, u32[]{:S(2)}) %collective-permute-start.20) | collective-permute-done | bytes 180256 | tf_op jit(solution)/shard_map/ppermute | solution.py:88
  76.3 8.0 %collective-permute-done.9 = bf16[2,1,2,128,256]{4,3,2,1,0:T(8,128)(2,1)S(1)} collective-permute-done((bf16[2,1,2,128,256]{4,3,2,1,0:T(8,128)(2,1)S(1)}, bf16[2,1,2,128,256]{4,3,2,1,0:T(8,128)(2,1)S(1)}, u32[]{:S(2)}, u32[]{:S(2)}) %collective-permute-start.9) | collective-permute-done | bytes 262176 | tf_op jit(solution)/shard_map/ppermute | solution.py:88
  100.9 11.9 %collective-permute-done.15 = bf16[2,1,2,128,256]{4,3,2,1,0:T(8,128)(2,1)} collective-permute-done((bf16[2,1,2,128,256]{4,3,2,1,0:T(8,128)(2,1)}, bf16[2,1,2,128,256]{4,3,2,1,0:T(8,128)(2,1)}, u32[]{:S(2)}, u32[]{:S(2)}) %collective-permute-start.15) | collective-permute-done | bytes 262176 | tf_op jit(solution)/shard_map/ppermute | solution.py:88
  151.4 5.4 collective-permute-done.22
  191.2 11.9 %convolution_convert_fusion.15 = bf16[64,4,512]{2,0,1:T(8,128)(2,1)S(1)} fusion(f32[1024,512,4]{1,0,2:T(8,128)S(1)} %get-tuple-element.189, f32[4,512]{1,0:T(4,128)S(1)} %log_add_fusion.3, pred[512,1024]{0,1:T(8,128)(4,1)S(1)} %iota_compare_fusion.1, bf16[1024,320]{0,1:T(8,128)(2,1)} %copy-done.83), kind=kOutput, calls=%fused_computation.116 | convolution fusion | flops 274857984 | bytes 9314304 | tf_op jit(solution)/shard_map/htu,ua->tha/dot_general | solution.py:52
  227.4 5.4 copy.278
  243.0 5.5 copy.254
  249.1 4.9 fusion.164
  264.2 5.2 multiply_reduce_fusion.1
  396.6 12.4 %collective-permute-done.68 = bf16[1,1,2,128,704]{3,4,2,1,0:T(8,128)(2,1)} collective-permute-done((bf16[1,1,2,128,704]{3,4,2,1,0:T(8,128)(2,1)}, bf16[1,1,2,128,704]{3,4,2,1,0:T(8,128)(2,1)}, u32[]{:S(2)}, u32[]{:S(2)}) %collective-permute-start.68) | collective-permute-done | bytes 360480 | tf_op jit(solution)/shard_map/ppermute | solution.py:88
  411.7 4.4 collective-permute-done.65
  453.8 5.4 fusion.120
  462.8 8.9 %fusion.3 = (f32[4,512]{1,0:T(4,128)S(1)}, f32[4,512]{1,0:T(4,128)S(1)}, f32[1024,512,4]{1,0,2:T(8,128)}) fusion(f32[1024,512,4]{1,0,2:T(8,128)S(1)} %bitcast.466, f32[4,512]{1,0:T(4,128)S(1)} %copy-done.146, pred[512,1024]{0,1:T(8,128)(4,1)S(1)} %copy-done.12, f32[1024,512,4]{1,0,2:T(8,128)} %fusion.120, f32[4,512]{1,0:T(4,128)S(1)} %copy-done.144, ...), kind=kOutput, calls=%fused_computation.11 | convolution fusion | flops 285208576 | bytes 34504704 | tf_op jit(solution)/shard_map/tha,ua->htu/dot_general | solution.py:69
  471.7 14.9 %fusion.5 = (bf16[4,512,1024]{1,2,0:T(8,128)(2,1)}, bf16[4,512,1024]{1,2,0:T(8,128)(2,1)S(1)}) fusion(f32[1024,512,4]{1,0,2:T(8,128)} %get-tuple-element.191, f32[1024,512,4]{1,0,2:T(8,128)} %copy-done.3, f32[4,512]{1,0:T(4,128)S(1)} %get-tuple-element.64, f32[4,512]{1,0:T(4,128)S(1)} %copy-done.146, pred[512,1024]{0,1:T(8,128)(4,1)} %copy-done.11, ...), kind=kLoop, calls=%fused_computation.13 | loop fusion | flops 20971520 | bytes 42500096 | tf_op jit(solution)/shard_map/convert_element_type | solution.py:71
  486.5 4.4 convolution_bitcast_fusion.5
  498.7 5.7 fusion.119
  504.5 8.7 %fusion = (f32[4,512]{1,0:T(4,128)S(1)}, f32[4,512]{1,0:T(4,128)S(1)}, f32[1024,512,4]{1,0,2:T(8,128)}) fusion(f32[1024,512,4]{1,0,2:T(8,128)S(1)} %bitcast.460, f32[4,512]{1,0:T(4,128)S(1)} %copy-done.140, pred[512,1024]{0,1:T(8,128)(4,1)S(1)} %copy-done.10, f32[1024,512,4]{1,0,2:T(8,128)} %fusion.119, f32[4,512]{1,0:T(4,128)S(1)} %copy-done.142, ...), kind=kOutput, calls=%fused_computation.6 | convolution fusion | flops 285208576 | bytes 34504704 | tf_op jit(solution)/shard_map/tha,ua->htu/dot_general | solution.py:69
  513.2 14.8 %fusion.2 = (bf16[4,512,1024]{1,2,0:T(8,128)(2,1)}, bf16[4,512,1024]{1,2,0:T(8,128)(2,1)S(1)}) fusion(f32[1024,512,4]{1,0,2:T(8,128)} %get-tuple-element.192, f32[1024,512,4]{1,0,2:T(8,128)} %copy-done.1, f32[4,512]{1,0:T(4,128)S(1)} %get-tuple-element.62, f32[4,512]{1,0:T(4,128)S(1)} %copy-done.140, pred[512,1024]{0,1:T(8,128)(4,1)S(1)} %copy-done.10, ...), kind=kLoop, calls=%fused_computation.8 | loop fusion | flops 20971520 | bytes 42500096 | tf_op jit(solution)/shard_map/convert_element_type | solution.py:71
  549.0 5.5 fusion.34
  585.6 7.6 %collective-permute-done.61 = bf16[1,1,2,128,256]{3,4,2,1,0:T(8,128)(2,1)S(1)} collective-permute-done((bf16[1,1,2,128,256]{3,4,2,1,0:T(8,128)(2,1)S(1)}, bf16[1,1,2,128,256]{3,4,2,1,0:T(8,128)(2,1)S(1)}, u32[]{:S(2)}, u32[]{:S(2)}) %collective-permute-start.61) | collective-permute-done | bytes 131104 | tf_op jit(solution)/shard_map/ppermute | solution.py:88
  596.7 6.1 collective-permute-done.58
  620.4 5.2 collective-permute-done.45
  652.8 9.1 %collective-permute-done.40 = bf16[256,1024]{0,1:T(8,128)(2,1)} collective-permute-done((bf16[256,1024]{0,1:T(8,128)(2,1)S(1)}, bf16[256,1024]{0,1:T(8,128)(2,1)}, u32[]{:S(2)}, u32[]{:S(2)}) %collective-permute-start.40) | collective-permute-done | bytes 524320 | tf_op jit(solution)/shard_map/ppermute | solution.py:79
  665.4 7.0 %collective-permute-done.35 = bf16[256,1024]{0,1:T(8,128)(2,1)} collective-permute-done((bf16[256,1024]{0,1:T(8,128)(2,1)S(1)}, bf16[256,1024]{0,1:T(8,128)(2,1)}, u32[]{:S(2)}, u32[]{:S(2)}) %collective-permute-start.35) | collective-permute-done | bytes 524320 | tf_op jit(solution)/shard_map/ppermute | solution.py:79
  (779 shorter events, 479.4 us)
Async XLA Ops:
  6.7 40.3 %collective-permute-start.30 = (bf16[1,1,1,128,704]{3,4,2,1,0:T(8,128)(2,1)}, bf16[1,1,1,128,704]{3,4,2,1,0:T(8,128)(2,1)}, u32[]{:S(2)}, u32[]{:S(2)}) collective-permute-start(bf16[1,1,1,128,704]{3,4,2,1,0:T(8,128)(2,1)} %bitcast.502), channel_id=1, source_target_pairs={{0,2},{1,3},{2,0},{3,1},{4,6},{5,7},{6,4},{7,5},{8,10},{9,11},{10,... | collective-permute-start | bytes 540680 | tf_op jit(solution)/shard_map/ppermute | solution.py:79
  7.2 36.8 %collective-permute-start.23 = (bf16[1,1,1,128,704]{3,4,2,1,0:T(8,128)(2,1)}, bf16[1,1,1,128,704]{3,4,2,1,0:T(8,128)(2,1)S(1)}, u32[]{:S(2)}, u32[]{:S(2)}) collective-permute-start(bf16[1,1,1,128,704]{3,4,2,1,0:T(8,128)(2,1)} %bitcast.503), channel_id=1, source_target_pairs={{0,4},{4,0},{8,12},{12,8},{16,20},{20,16},{24,28},{28,24},{1,5},{5... | collective-permute-start | bytes 540680 | tf_op jit(solution)/shard_map/ppermute | solution.py:88
  25.4 60.6 %collective-permute-start = (bf16[256,1024]{0,1:T(8,128)(2,1)}, bf16[256,1024]{0,1:T(8,128)(2,1)S(1)}, u32[]{:S(2)}, u32[]{:S(2)}) collective-permute-start(bf16[256,1024]{0,1:T(8,128)(2,1)} %bitcast.1), channel_id=1, source_target_pairs={{0,2},{1,3},{2,0},{3,1},{4,6},{5,7},{6,4},{7,5},{8,10},{9,11},{10,... | collective-permute-start | bytes 1572872 | tf_op jit(solution)/shard_map/ppermute | solution.py:79
  28.4 60.4 %collective-permute-start.36 = (bf16[256,1024]{0,1:T(8,128)(2,1)}, bf16[256,1024]{0,1:T(8,128)(2,1)}, u32[]{:S(2)}, u32[]{:S(2)}) collective-permute-start(bf16[256,1024]{0,1:T(8,128)(2,1)} %bitcast.59), channel_id=1, source_target_pairs={{0,2},{1,3},{2,0},{3,1},{4,6},{5,7},{6,4},{7,5},{8,10},{9,11},{10,... | collective-permute-start | bytes 1572872 | tf_op jit(solution)/shard_map/ppermute | solution.py:79
  75.3 39.1 %collective-permute-start.18 = (bf16[2,1,1,128,704]{3,4,2,1,0:T(8,128)(2,1)}, bf16[2,1,1,128,704]{3,4,2,1,0:T(8,128)(2,1)}, u32[]{:S(2)}, u32[]{:S(2)}) collective-permute-start(bf16[2,1,1,128,704]{3,4,2,1,0:T(8,128)(2,1)} %pad_maximum_fusion.27), channel_id=1, source_target_pairs={{0,8},{4,12},{8,0},{12,4},{16,24},{20,28},{24,16},{28,20},{1,9},{5... | collective-permute-start | bytes 1081352 | tf_op jit(solution)/shard_map/ppermute | solution.py:88
  84.3 35.8 %collective-permute-start.21 = (bf16[2,1,1,128,704]{3,4,2,1,0:T(8,128)(2,1)}, bf16[2,1,1,128,704]{3,4,2,1,0:T(8,128)(2,1)}, u32[]{:S(2)}, u32[]{:S(2)}) collective-permute-start(bf16[2,1,1,128,704]{3,4,2,1,0:T(8,128)(2,1)} %pad_maximum_fusion.28), channel_id=1, source_target_pairs={{0,8},{4,12},{8,0},{12,4},{16,24},{20,28},{24,16},{28,20},{1,9},{5... | collective-permute-start | bytes 1081352 | tf_op jit(solution)/shard_map/ppermute | solution.py:88
  97.1 36.4 %collective-permute-start.25 = (bf16[2,1,2,128,704]{3,4,2,1,0:T(8,128)(2,1)}, bf16[2,1,2,128,704]{3,4,2,1,0:T(8,128)(2,1)}, u32[]{:S(2)}, u32[]{:S(2)}) collective-permute-start(bf16[2,1,2,128,704]{3,4,2,1,0:T(8,128)(2,1)} %pad_maximum_fusion.14), channel_id=1, source_target_pairs={{0,8},{4,12},{8,0},{12,4},{16,24},{20,28},{24,16},{28,20},{1,9},{5... | collective-permute-start | bytes 2162696 | tf_op jit(solution)/shard_map/ppermute | solution.py:88
  120.1 45.2 %collective-permute-start.1 = (bf16[2,256,1024]{1,2,0:T(8,128)(2,1)S(1)}, bf16[2,256,1024]{1,2,0:T(8,128)(2,1)}, u32[]{:S(2)}, u32[]{:S(2)}) collective-permute-start(bf16[2,256,1024]{1,2,0:T(8,128)(2,1)S(1)} %bitcast.482), channel_id=1, source_target_pairs={{0,1},{1,0},{2,3},{3,2},{4,5},{5,4},{6,7},{7,6},{8,9},{9,8},{10,11... | collective-permute-start | bytes 3145736 | tf_op jit(solution)/shard_map/ppermute | solution.py:83
  146.4 76.2 %collective-permute-start.37 = (bf16[2,256,1024]{1,2,0:T(8,128)(2,1)}, bf16[2,256,1024]{1,2,0:T(8,128)(2,1)}, u32[]{:S(2)}, u32[]{:S(2)}) collective-permute-start(bf16[2,256,1024]{1,2,0:T(8,128)(2,1)} %bitcast.63), channel_id=1, source_target_pairs={{0,1},{1,0},{2,3},{3,2},{4,5},{5,4},{6,7},{7,6},{8,9},{9,8},{10,11... | collective-permute-start | bytes 3145736 | tf_op jit(solution)/shard_map/ppermute | solution.py:83
  156.8 60.7 %collective-permute-start.33 = (bf16[2,1,2,128,704]{3,4,2,1,0:T(8,128)(2,1)}, bf16[2,1,2,128,704]{3,4,2,1,0:T(8,128)(2,1)}, u32[]{:S(2)}, u32[]{:S(2)}) collective-permute-start(bf16[2,1,2,128,704]{3,4,2,1,0:T(8,128)(2,1)} %pad_maximum_fusion.15), channel_id=1, source_target_pairs={{0,8},{4,12},{8,0},{12,4},{16,24},{20,28},{24,16},{28,20},{1,9},{5... | collective-permute-start | bytes 2162696 | tf_op jit(solution)/shard_map/ppermute | solution.py:88
  163.3 90.7 %collective-permute-start.27 = (bf16[2,2,1,128,704]{3,4,2,1,0:T(8,128)(2,1)}, bf16[2,2,1,128,704]{3,4,2,1,0:T(8,128)(2,1)}, u32[]{:S(2)}, u32[]{:S(2)}) collective-permute-start(bf16[2,2,1,128,704]{3,4,2,1,0:T(8,128)(2,1)} %collective-permute-done.26), channel_id=1, source_target_pairs={{0,4},{4,0},{8,12},{12,8},{16,20},{20,16},{24,28},{28,24},{1,5},{5... | collective-permute-start | bytes 2162696 | tf_op jit(solution)/shard_map/ppermute | solution.py:88
  164.3 94.6 %collective-permute-start.29 = (bf16[2,2,1,128,704]{3,4,2,1,0:T(8,128)(2,1)}, bf16[2,2,1,128,704]{3,4,2,1,0:T(8,128)(2,1)}, u32[]{:S(2)}, u32[]{:S(2)}) collective-permute-start(bf16[2,2,1,128,704]{3,4,2,1,0:T(8,128)(2,1)} %collective-permute-done.28), channel_id=1, source_target_pairs={{0,4},{4,0},{8,12},{12,8},{16,20},{20,16},{24,28},{28,24},{1,5},{5... | collective-permute-start | bytes 2162696 | tf_op jit(solution)/shard_map/ppermute | solution.py:88
  217.4 46.8 %collective-permute-start.16 = (bf16[1024,1024]{1,0:T(8,128)(2,1)S(1)}, bf16[1024,1024]{1,0:T(8,128)(2,1)}, u32[]{:S(2)}, u32[]{:S(2)}) collective-permute-start(bf16[1024,1024]{1,0:T(8,128)(2,1)S(1)} %add_convert_fusion.3), channel_id=1, source_target_pairs={{0,1},{1,0},{2,3},{3,2},{4,5},{5,4},{6,7},{7,6},{8,9},{9,8},{10,11... | collective-permute-start | bytes 6291464 | tf_op jit(solution)/shard_map/ppermute | solution.py:83
  322.2 53.2 %collective-permute-start.67 = (bf16[2,1,2,128,704]{3,4,2,1,0:T(8,128)(2,1)}, bf16[2,1,2,128,704]{3,4,2,1,0:T(8,128)(2,1)}, u32[]{:S(2)}, u32[]{:S(2)}) collective-permute-start(bf16[2,1,2,128,704]{3,4,2,1,0:T(8,128)(2,1)} %copy.353), channel_id=1, source_target_pairs={{0,8},{4,12},{8,0},{12,4},{16,24},{20,28},{24,16},{28,20},{1,9},{5... | collective-permute-start | bytes 2162696 | tf_op jit(solution)/shard_map/ppermute | solution.py:88
  329.4 49.1 %collective-permute-start.51 = (bf16[2,2,1,128,704]{3,4,2,1,0:T(8,128)(2,1)}, bf16[2,2,1,128,704]{3,4,2,1,0:T(8,128)(2,1)}, u32[]{:S(2)}, u32[]{:S(2)}) collective-permute-start(bf16[2,2,1,128,704]{3,4,2,1,0:T(8,128)(2,1)} %copy.345), channel_id=1, source_target_pairs={{0,4},{4,0},{8,12},{12,8},{16,20},{20,16},{24,28},{28,24},{1,5},{5... | collective-permute-start | bytes 2162696 | tf_op jit(solution)/shard_map/ppermute | solution.py:88
  330.2 99.2 %collective-permute-start.46 = (bf16[2,2,2,128,704]{3,4,2,1,0:T(8,128)(2,1)}, bf16[2,2,2,128,704]{3,4,2,1,0:T(8,128)(2,1)}, u32[]{:S(2)}, u32[]{:S(2)}) collective-permute-start(bf16[2,2,2,128,704]{3,4,2,1,0:T(8,128)(2,1)} %copy.303), channel_id=1, source_target_pairs={{0,2},{1,3},{2,0},{3,1},{4,6},{5,7},{6,4},{7,5},{8,10},{9,11},{10,... | collective-permute-start | bytes 4325384 | tf_op jit(solution)/shard_map/ppermute | solution.py:79
  342.1 39.0 %collective-permute-start.64 = (bf16[2,1,2,128,704]{3,4,2,1,0:T(8,128)(2,1)}, bf16[2,1,2,128,704]{3,4,2,1,0:T(8,128)(2,1)}, u32[]{:S(2)}, u32[]{:S(2)}) collective-permute-start(bf16[2,1,2,128,704]{3,4,2,1,0:T(8,128)(2,1)} %copy.351), channel_id=1, source_target_pairs={{0,8},{4,12},{8,0},{12,4},{16,24},{20,28},{24,16},{28,20},{1,9},{5... | collective-permute-start | bytes 2162696 | tf_op jit(solution)/shard_map/ppermute | solution.py:88
  344.7 40.7 %collective-permute-start.34 = (bf16[2,256,1024]{1,2,0:T(8,128)(2,1)}, bf16[2,256,1024]{1,2,0:T(8,128)(2,1)}, u32[]{:S(2)}, u32[]{:S(2)}) collective-permute-start(bf16[2,256,1024]{1,2,0:T(8,128)(2,1)} %bitcast.50), channel_id=1, source_target_pairs={{0,1},{1,0},{2,3},{3,2},{4,5},{5,4},{6,7},{7,6},{8,9},{9,8},{10,11... | collective-permute-start | bytes 3145736 | tf_op jit(solution)/shard_map/ppermute | solution.py:83
  375.3 47.5 %collective-permute-start.50 = (bf16[2,2,1,128,704]{3,4,2,1,0:T(8,128)(2,1)}, bf16[2,2,1,128,704]{3,4,2,1,0:T(8,128)(2,1)}, u32[]{:S(2)}, u32[]{:S(2)}) collective-permute-start(bf16[2,2,1,128,704]{3,4,2,1,0:T(8,128)(2,1)} %copy.343), channel_id=1, source_target_pairs={{0,4},{4,0},{8,12},{12,8},{16,20},{20,16},{24,28},{28,24},{1,5},{5... | collective-permute-start | bytes 2162696 | tf_op jit(solution)/shard_map/ppermute | solution.py:88
  378.6 59.9 %collective-permute-start.38 = (bf16[1024,1024]{1,0:T(8,128)(2,1)S(1)}, bf16[1024,1024]{1,0:T(8,128)(2,1)}, u32[]{:S(2)}, u32[]{:S(2)}) collective-permute-start(bf16[1024,1024]{1,0:T(8,128)(2,1)S(1)} %add_convert_fusion.1), channel_id=1, source_target_pairs={{0,1},{1,0},{2,3},{3,2},{4,5},{5,4},{6,7},{7,6},{8,9},{9,8},{10,11... | collective-permute-start | bytes 6291464 | tf_op jit(solution)/shard_map/ppermute | solution.py:83
  432.3 144.6 %collective-permute-start.47 = (bf16[2,2,1,128,704]{3,4,2,1,0:T(8,128)(2,1)}, bf16[2,2,1,128,704]{3,4,2,1,0:T(8,128)(2,1)}, u32[]{:S(2)}, u32[]{:S(2)}) collective-permute-start(bf16[2,2,1,128,704]{3,4,2,1,0:T(8,128)(2,1)} %slice.434), channel_id=1, source_target_pairs={{0,4},{4,0},{8,12},{12,8},{16,20},{20,16},{24,28},{28,24},{1,5},{5... | collective-permute-start | bytes 2162696 | tf_op jit(solution)/shard_map/ppermute | solution.py:88
  438.3 173.9 %collective-permute-start.54 = (bf16[1,1,1,128,704]{3,4,2,1,0:T(8,128)(2,1)}, bf16[1,1,1,128,704]{3,4,2,1,0:T(8,128)(2,1)}, u32[]{:S(2)}, u32[]{:S(2)}) collective-permute-start(bf16[1,1,1,128,704]{3,4,2,1,0:T(8,128)(2,1)} %slice.446), channel_id=1, source_target_pairs={{0,16},{4,20},{8,24},{12,28},{16,0},{20,4},{24,8},{28,12},{1,17},{... | collective-permute-start | bytes 540680 | tf_op jit(solution)/shard_map/ppermute | solution.py:88
  545.6 33.8 %collective-permute-start.60 = (bf16[2,1,2,128,256]{3,4,2,1,0:T(8,128)(2,1)}, bf16[2,1,2,128,256]{3,4,2,1,0:T(8,128)(2,1)}, u32[]{:S(2)}, u32[]{:S(2)}) collective-permute-start(bf16[2,1,2,128,256]{3,4,2,1,0:T(8,128)(2,1)} %copy.349), channel_id=1, source_target_pairs={{0,8},{4,12},{8,0},{12,4},{16,24},{20,28},{24,16},{28,20},{1,9},{5... | collective-permute-start | bytes 786440 | tf_op jit(solution)/shard_map/ppermute | solution.py:88
  579.4 49.0 %collective-permute-start.39 = (bf16[2,256,1024]{1,2,0:T(8,128)(2,1)}, bf16[2,256,1024]{1,2,0:T(8,128)(2,1)}, u32[]{:S(2)}, u32[]{:S(2)}) collective-permute-start(bf16[2,256,1024]{1,2,0:T(8,128)(2,1)} %bitcast.96), channel_id=1, source_target_pairs={{0,1},{1,0},{2,3},{3,2},{4,5},{5,4},{6,7},{7,6},{8,9},{9,8},{10,11... | collective-permute-start | bytes 3145736 | tf_op jit(solution)/shard_map/ppermute | solution.py:83
  (233 other events, 3009.0 us)
